TPU v7x, 256 devices: a whole 4x4x8 slice. The times are simulated.
256 devices in a mesh: outer: 16 (over y, x), inner: 16 (over z, core).
Axes of the slice: x: 4, y: 4, z: 8, core: 2. Of those that a mesh axis runs over, the one named last changes fastest.
Arguments:
- tokens: bfloat16 [65536, 8192], P(('outer', 'inner')), may hold values from -24 to 24
- upstream: bfloat16 [65536, 8192], P(('outer', 'inner')), may hold values from -24 to 24
- weights: bfloat16 [3, 8192, 256], P(None, ('outer', 'inner')), may hold values from -0.0625 to 0.0625
Outputs:
- gradients: float32 [3, 256, 8192], P(None, 'inner', 'outer')
All inputs are finite; a program needn't handle non-finite values.
Results may differ from a plain program's by a relative error of at most 0.0049.
Values may be sent and summed in bfloat16 or wider, within the bound.
A program may use at most 128 MiB of HBM per device.

v0:
```python
import jax
import jax.numpy as jnp
from jax import lax
from jax.sharding import PartitionSpec as P


def cut_along(value, dim, size):
    before, after = (value.shape[:dim], value.shape[dim + 1 :])
    return jnp.moveaxis(value.reshape(*before, size, -1, *after), dim, 0)


def piece_ends(length, count):
    step = length // count
    if step >= 8:
        step -= step % 8
    return [step * k for k in range(1, count)]


def in_order(tiles, dim):
    tiles = jnp.moveaxis(tiles, 0, dim)
    shape = tiles.shape
    return tiles.reshape(*shape[:dim], shape[dim] * shape[dim + 1], *shape[dim + 2 :])


def exchange_in_pieces(value, axis, pieces, split_dim, concat_dim):
    tiles = cut_along(value, split_dim, lax.axis_size(axis))
    cut = max(range(1, max(2, tiles.ndim - 1)), key=lambda d: tiles.shape[d])
    done = []
    for share in jnp.split(tiles, piece_ends(tiles.shape[cut], pieces), axis=cut):
        if share.size:
            done.append(lax.all_to_all(share, axis, split_axis=0, concat_axis=0, tiled=True))
    return in_order(jnp.concatenate(done, axis=cut), concat_dim)


def combine_received(received):
    return jnp.sum(received.astype(jnp.float32), axis=0)


def on_device(tokens, upstream, weights):
    full_weights = lax.all_gather(weights, ("outer", "inner"), axis=1, tiled=True)
    gate_pre = jnp.dot(tokens, full_weights[0], preferred_element_type=jnp.float32)
    up_pre = jnp.dot(tokens, full_weights[1], preferred_element_type=jnp.float32)
    hidden_grad = jnp.dot(upstream, full_weights[2], preferred_element_type=jnp.float32)
    sigmoid = jax.nn.sigmoid(gate_pre)
    activated = gate_pre * sigmoid
    hidden = (activated * up_pre).astype(jnp.bfloat16)
    grad_gate = (hidden_grad * up_pre * sigmoid * (1.0 + gate_pre * (1.0 - sigmoid))).astype(
        jnp.bfloat16
    )
    grad_up = (hidden_grad * activated).astype(jnp.bfloat16)
    stacked = jnp.stack(
        [
            jnp.dot(grad_gate.T, tokens, preferred_element_type=jnp.float32),
            jnp.dot(grad_up.T, tokens, preferred_element_type=jnp.float32),
            jnp.dot(hidden.T, upstream, preferred_element_type=jnp.float32),
        ]
    ).astype(jnp.bfloat16)
    received = exchange_in_pieces(stacked[None], "inner", 2, 2, 0)
    partial_sum = combine_received(received)
    partial_rounded = partial_sum.astype(jnp.bfloat16)
    final_pieces = lax.all_to_all(
        partial_rounded[None], "outer", split_axis=3, concat_axis=0, tiled=True
    )
    return combine_received(final_pieces)


def solution(mesh):
    placed = (
        P(("outer", "inner"), None),
        P(("outer", "inner"), None),
        P(None, ("outer", "inner"), None),
    )
    return jax.shard_map(
        on_device, mesh=mesh, in_specs=placed, out_specs=P(None, "inner", "outer"), check_vma=False
    )
```

profile of v0, /device:TPU:32, one launch (start us, length us, event | category | flops | bytes accessed | tf_op | source)
XLA Modules:
  0.0 514.3 jit_solution(4578464147569142469)
XLA Ops:
  6.5 0.0 all-gather.2.cloned.1.call-start
  6.5 0.7 all-gather.2.cloned.1.call-update
  7.3 127.5 %all-gather.2.cloned.1.call-done = bf16[3,8192,256]{2,1,0:T(8,128)(2,1)} async-done(((bf16[3,32,256]{2,1,0:T(8,128)(2,1)}), bf16[3,8192,256]{2,1,0:T(8,128)(2,1)}) %all-gather.2.cloned.1.call-update) | async-done | bytes 12582928 | tf_op jit(solution)/shard_map/all_gather | solution.py:40
  134.7 0.0 copy-start.1
  134.7 4.8 fusion
  139.6 0.0 copy-done.1
  139.6 0.0 copy-start
  139.6 3.6 fusion.2
  143.2 0.0 copy-done
  143.2 1.3 convolution_convert_fusion.1
  144.5 3.4 fusion.1
  147.9 1.4 convolution_convert_fusion.2
  149.3 1.3 convolution_convert_fusion
  150.6 1.6 maximum_bitcast_fusion
  152.2 1.3 fusion.10
  153.6 143.1 %all_to_all.19 = bf16[16,1,3,8,8192]{4,3,2,1,0:T(8,128)(2,1)} all-to-all(bf16[16,1,3,8,8192]{4,3,2,1,0:T(8,128)(2,1)S(1)} %get-tuple-element.5), channel_id=1, replica_groups=mesh['outer'=16,'inner'=16] {'inner'}, dimensions={0} | all-to-all | bytes 12582912 | tf_op jit(solution)/shard_map/all_to_all | solution.py:31
  296.7 143.9 %all_to_all.20 = bf16[16,1,3,8,8192]{4,3,2,1,0:T(8,128)(2,1)} all-to-all(bf16[16,1,3,8,8192]{4,3,2,1,0:T(8,128)(2,1)S(1)} %get-tuple-element.6), channel_id=1, replica_groups=mesh['outer'=16,'inner'=16] {'inner'}, dimensions={0} | all-to-all | bytes 12582912 | tf_op jit(solution)/shard_map/all_to_all | solution.py:31
  440.6 6.6 %maximum_reduce_fusion = bf16[3,16,8192]{2,1,0:T(8,128)(2,1)S(1)} fusion(bf16[16,1,3,8,8192]{4,3,2,1,0:T(8,128)(2,1)} %all_to_all.20, bf16[16,1,3,8,8192]{4,3,2,1,0:T(8,128)(2,1)} %all_to_all.19), kind=kLoop, calls=%fused_computation.2 | loop fusion | flops 31064064 | bytes 13369344 | tf_op jit(solution)/shard_map/reduce_sum | solution.py:36
  447.2 8.3 %copy.10 = bf16[1,3,16,8192]{2,1,0,3:T(4,128)(2,1)} copy(bf16[1,3,16,8192]{3,2,1,0:T(8,128)(2,1)S(1)} %bitcast.36) | data formatting | bytes 1572864 | tf_op jit(solution)/shard_map/broadcast_in_dim | solution.py:62
  455.5 12.8 %reshape.54 = bf16[16,2,12288]{2,1,0:T(2,128)(2,1)S(1)} reshape(bf16[8192,1,3,16]{3,2,1,0:T(4,128)(2,1)} %bitcast.31) | data formatting | bytes 1572864
  468.3 19.3 %all_to_all.21 = bf16[16,2,12288]{2,1,0:T(2,128)(2,1)S(1)} all-to-all(bf16[16,2,12288]{2,1,0:T(2,128)(2,1)S(1)} %reshape.54), channel_id=1, replica_groups=mesh['outer'=16,'inner'=16] {'outer'}, dimensions={0} | all-to-all | bytes 1572864 | tf_op jit(solution)/shard_map/all_to_all | solution.py:61
  487.6 10.7 %reshape.55 = bf16[8192,1,3,16]{3,2,1,0:T(4,128)(2,1)} reshape(bf16[16,2,12288]{2,1,0:T(2,128)(2,1)S(1)} %all_to_all.21) | data formatting | bytes 1572864
  498.4 8.1 %convert_reduce_fusion = f32[3,16,512]{1,0,2:T(4,128)S(1)} fusion(bf16[3,16,16,512]{1,0,3,2:T(4,128)(2,1)} %bitcast.32), kind=kLoop, calls=%fused_computation | loop fusion | flops 761856 | bytes 884736 | tf_op jit(solution)/shard_map/reduce_sum | solution.py:36
  506.5 0.9 copy.11
Async XLA Ops:
  6.5 128.2 %all-gather.2.cloned.1.call-start = ((), (), s32[]{:S(2)}) async-start(), calls=%async_computation.3 | async-start | bytes 12632064 | tf_op jit(solution)/shard_map/all_gather | solution.py:40
  134.7 4.9 copy-start.1
  139.6 3.6 copy-start
Sparse Core Ops, SparseCore 0:
  11.0 123.6 all-gather.1
where the time goes:
time: 518 us; the launch traced here: 514 us
  blocking collectives  306 us (59%)
  waiting for transfers between devices  128 us (25%)
  local copies, waits for them, and re-layouts  34.1 us (7%)
  other arithmetic  16.4 us (3%)
  matrix products  15.8 us (3%)
  between operations  13.5 us (3%)
    all_to_all x2, blocking collectives, exchange_in_pieces(): lax.all_to_all(share, axis, split_axis=0, concat_axis=0, tiled=True)  287 us
    all_gather x1, waiting for transfers between devices, on_device(): lax.all_gather(weights, ('outer', 'inner'), axis=1, tiled=True)  127 us
    unnamed x6, local copies, waits for them, and re-layouts  23.6 us
    all_to_all x1, blocking collectives, on_device(): lax.all_to_all(partial_rounded[None], 'outer', split_axis=3, concat_axis=...  19.3 us
    reduce_sum x2, other arithmetic, combine_received(): return jnp.sum(received.astype(jnp.float32), axis=0)  14.8 us
  transfers between devices with their start and end apart: 1, of which 1 were waited for; matrix products, arithmetic and copies ran while one was open for 0% of the time, Pallas kernels for 0%

commit v1 on v0

v1 whole, which is shorter than its diff:
```python
import jax
import jax.numpy as jnp
from jax import lax
from jax.experimental import pallas as pl
from jax.experimental.pallas import tpu as pltpu
from jax.sharding import PartitionSpec as P

MESH = pl.DeviceIdType.MESH
BF16, F32 = jnp.bfloat16, jnp.float32
NX, NY, NZ = 4, 4, 8
COLS = 512
HALF = COLS // 2
UNITS = 128
TOK = 256
MODEL = 8192


def place(x, y, z, c):
    return (y * NX + x, z * 2 + c)


class Links:
    def __init__(self, send_sems, recv_sems):
        self.send_sems, self.recv_sems = send_sems, recv_sems
        self.count = 0
        self.started = []

    def send(self, src, dst, target):
        k = self.count
        self.count += 1
        copy = pltpu.make_async_remote_copy(
            src_ref=src,
            dst_ref=dst,
            send_sem=self.send_sems.at[k],
            recv_sem=self.recv_sems.at[k],
            device_id=target,
            device_id_type=MESH,
        )
        copy.start()
        self.started.append(copy)
        return copy

    def drain(self):
        for copy in self.started:
            copy.wait_send()


N_COPIES = 256


def kernel(
    tokens,
    upstream,
    shard,
    out,
    tok,
    ups,
    full,
    stage,
    grads,
    down,
    sent1,
    got1,
    part1,
    sent2,
    got2,
    sent3,
    got3,
    zsent,
    zgot,
    zpart,
    ysent,
    ygot,
    xsent,
    xgot,
    send_sems,
    recv_sems,
    local_sems,
):
    links = Links(send_sems, recv_sems)
    outer, inner = lax.axis_index("outer"), lax.axis_index("inner")
    x, y = lax.rem(outer, NX), lax.div(outer, NX)
    z, c = lax.div(inner, 2), lax.rem(inner, 2)

    def at_x(d):
        return lax.rem(x + d + NX, NX)

    def at_y(d):
        return lax.rem(y + d + NY, NY)

    def at_z(d):
        return lax.rem(z + d + NZ, NZ)

    def to_x(d):
        return place(at_x(d), y, z, c)

    def to_y(d):
        return place(x, at_y(d), z, c)

    def to_z(d):
        return place(x, y, at_z(d), c)

    sibling = place(x, y, z, 1 - c)

    load_tok = pltpu.make_async_copy(tokens, tok.at[pl.ds(0, TOK)], local_sems.at[0])
    load_ups = pltpu.make_async_copy(upstream, ups.at[pl.ds(0, TOK)], local_sems.at[1])
    load_tok.start()
    load_ups.start()

    barrier = pltpu.get_barrier_semaphore()
    partners = [sibling]
    partners += [to_x(d) for d in (1, 2, 3)]
    partners += [to_y(d) for d in (1, 3)]
    partners += [to_z(d) for d in range(1, NZ)]
    for partner in partners:
        pl.semaphore_signal(barrier, inc=1, device_id=partner, device_id_type=MESH)

    row = lax.broadcasted_iota(jnp.int32, (256, 256), 0)
    lane = lax.broadcasted_iota(jnp.int32, (256, 256), 1)
    slot = lane % UNITS
    half = jnp.where(lane < UNITS, c, 1 - c)
    pick = (row == (slot // 16) * 32 + half * 16 + slot % 16).astype(F32).astype(BF16)
    home = y * NX + x
    for m in range(3):
        moved = jnp.dot(shard[m], pick, preferred_element_type=F32).astype(BF16)
        full[m, home, z, pl.ds(pl.multiple_of(c * 32, 32), 32), :] = moved[:, :UNITS]
        stage[m] = moved[:, UNITS:]
    pl.semaphore_wait(barrier, len(partners))

    swap = [
        links.send(
            stage.at[m],
            full.at[m, home, z, pl.ds(pl.multiple_of(c * 32, 32), 32)],
            sibling,
        )
        for m in range(3)
    ]
    for copy in swap:
        copy.wait_recv()
    near = (1, 7, 2, 6, 3, 5, 4)
    block0, block1, block2 = (full.at[m, home, z] for m in range(3))
    a_z = [links.send(block0, block0, to_z(d)) for d in near]
    c_x = [links.send(block2, block2, to_x(d)) for d in (1, 3, 2)]
    b_z = [links.send(block1, block1, to_z(d)) for d in near]
    tok_copy = links.send(tokens, tok.at[pl.ds(TOK, TOK)], sibling)
    ups_copy = links.send(upstream, ups.at[pl.ds(TOK, TOK)], sibling)

    def wait_all(copies):
        for copy in copies:
            copy.wait_recv()

    def plane(yy, zz, x0=0, n=NX):
        return full.at[2, pl.ds(yy * NX + x0, n), zz]

    class Ring4:
        def __init__(self, whole, part, to):
            self.whole, self.part, self.to = whole, part, to

        def first(self):
            ref = self.whole(0)
            self.hop1 = (
                links.send(ref, ref, self.to(1)),
                links.send(ref, ref, self.to(-1)),
            )

        def forward(self):
            wait_all(self.hop1)
            right, left = self.part(-1, 0), self.part(1, 1)
            self.hop2 = (
                links.send(right, right, self.to(1)),
                links.send(left, left, self.to(-1)),
            )

        def finish(self):
            wait_all(self.hop2)

    def piece(m, yy, xx, h=None):
        ref = full.at[m, yy * NX + xx]
        return ref if h is None else ref.at[pl.ds(h * 4, 4)]

    a_y = Ring4(lambda d: piece(0, at_y(d), x), lambda d, h: piece(0, at_y(d), x, h), to_y)
    b_x = Ring4(lambda d: piece(1, y, at_x(d)), lambda d, h: piece(1, y, at_x(d), h), to_x)
    c_y = Ring4(lambda d: plane(at_y(d), z), lambda d, h: plane(at_y(d), z, 2 * h, 2), to_y)

    def a_bulk(g):
        return Ring4(
            lambda d: piece(0, at_y(g), at_x(d)), lambda d, h: piece(0, at_y(g), at_x(d), h), to_x
        )

    def b_bulk(g):
        return Ring4(
            lambda d: piece(1, at_y(d), at_x(g)), lambda d, h: piece(1, at_y(d), at_x(g), h), to_y
        )

    class Ring8:
        def __init__(self, g, long_way):
            self.g, self.hops = g, {1: 4 if long_way == 1 else 3, -1: 4 if long_way == -1 else 3}
            self.last = {}

        def hop(self, h):
            for way in (1, -1):
                if h <= self.hops[way]:
                    if h > 1:
                        self.last[way].wait_recv()
                    ref = plane(at_y(self.g), at_z(-way * (h - 1)))
                    self.last[way] = links.send(ref, ref, to_z(way))

        def finish(self):
            wait_all(self.last.values())

    cz = {g: Ring8(g, 1 if k % 2 == 0 else -1) for k, g in enumerate((0, 1, -1, 2))}
    ax = {g: a_bulk(g) for g in (0, 1, -1, 2)}
    by = {g: b_bulk(g) for g in (0, 1, -1, 2)}

    wait_all(c_x)
    c_y.first()
    cz[0].hop(1)
    wait_all(a_z)
    a_y.first()
    ax[0].first()
    c_y.forward()
    cz[1].hop(1)
    cz[-1].hop(1)
    wait_all(b_z)
    b_x.first()
    by[0].first()
    c_y.finish()
    cz[2].hop(1)
    cz[0].hop(2)
    a_y.forward()
    ax[1].first()
    ax[-1].first()
    b_x.forward()
    by[1].first()
    by[-1].first()
    cz[1].hop(2)
    cz[-1].hop(2)
    ax[0].forward()
    by[0].forward()
    cz[0].hop(3)
    cz[2].hop(2)
    a_y.finish()
    ax[2].first()
    b_x.finish()
    by[2].first()
    cz[1].hop(3)
    cz[-1].hop(3)
    cz[0].hop(4)
    ax[1].forward()
    ax[-1].forward()
    by[1].forward()
    by[-1].forward()
    cz[2].hop(3)
    cz[1].hop(4)
    cz[-1].hop(4)
    ax[2].forward()
    by[2].forward()
    cz[2].hop(4)

    load_tok.wait()
    load_ups.wait()
    tok_copy.wait_recv()

    def forward(m, source):
        def step(k, total):
            rows = pl.ds(pl.multiple_of(k * COLS, COLS), COLS)
            block = full[m, k].reshape(COLS, UNITS)
            return total + jnp.dot(source[:, rows], block, preferred_element_type=F32)

        return lax.fori_loop(0, NX * NY, step, jnp.zeros((2 * TOK, UNITS), F32))

    for g in (0, 1, -1, 2):
        ax[g].finish()
    gate = forward(0, tok)
    for g in (0, 1, -1, 2):
        by[g].finish()
    up = forward(1, tok)
    sigmoid = jax.nn.sigmoid(gate)
    activated = gate * sigmoid
    ups_copy.wait_recv()
    for g in (0, 1, -1, 2):
        cz[g].finish()
    hidden_grad = forward(2, ups)
    hidden = activated * up
    grad_gate = hidden_grad * up * sigmoid * (1.0 + gate * (1.0 - sigmoid))
    grad_up = hidden_grad * activated
    grads[0] = grad_gate.T.astype(BF16)
    grads[1] = grad_up.T.astype(BF16)
    grads[2] = hidden.T.astype(BF16)

    def term(m, yy, xx, h):
        start = pl.multiple_of((yy * NX + xx) * COLS + h * HALF, HALF)
        return jnp.dot(grads[m], tok[:, pl.ds(start, HALF)], preferred_element_type=F32)

    class Fold4:
        def __init__(self, own, sent, got, to):
            self.own, self.sent, self.got, self.to = own, sent, got, to

        def put(self, k, value, way):
            self.sent[k] = value.astype(BF16)
            return links.send(self.sent.at[k], self.got.at[k], self.to(way))

        def far(self):
            self.c0 = self.put(0, self.own(2, 0), 1)
            self.c1 = self.put(1, self.own(2, 1), -1)

        def right(self):
            self.c2 = self.put(2, self.own(1, 1), 1)

        def left(self):
            self.c3 = self.put(3, self.own(-1, 0), -1)

        def relay_right(self):
            self.c0.wait_recv()
            self.c4 = self.put(4, self.own(1, 0) + self.got[0].astype(F32), 1)

        def relay_left(self):
            self.c1.wait_recv()
            self.c5 = self.put(5, self.own(-1, 1) + self.got[1].astype(F32), -1)

        def total(self):
            wait_all((self.c2, self.c3, self.c4, self.c5))
            first = self.own(0, 0) + self.got[4].astype(F32) + self.got[3].astype(F32)
            second = self.own(0, 1) + self.got[2].astype(F32) + self.got[5].astype(F32)
            return first, second

    order = (2, 1, -1, 0)

    def a_fold(k, g):
        return Fold4(
            lambda d, h: term(0, at_y(g), at_x(d), h), sent1.at[0, k], got1.at[0, k], to_x
        )

    def b_fold(k, g):
        return Fold4(
            lambda d, h: term(1, at_y(d), at_x(g), h), sent1.at[1, k], got1.at[1, k], to_y
        )

    folds = [[a_fold(k, g) for k, g in enumerate(order)], [b_fold(k, g) for k, g in enumerate(order)]]
    index = {g: k for k, g in enumerate(order)}

    def half_ref(m, d, h):
        return part1[m, index[2 if d == -2 else d], :, h * HALF : (h + 1) * HALF]

    folds2 = [
        Fold4(lambda d, h: half_ref(0, d, h), sent2.at[0], got2.at[0], to_y),
        Fold4(lambda d, h: half_ref(1, d, h), sent2.at[1], got2.at[1], to_x),
    ]

    def now(k):
        for fold in (folds[0][k], folds[1][k]):
            fold.far()
            fold.right()
            fold.left()

    def relay(k):
        for fold in (folds[0][k], folds[1][k]):
            fold.relay_right()
            fold.relay_left()

    def close(k):
        for m in range(2):
            first, second = folds[m][k].total()
            part1[m, k, :, :HALF] = first
            part1[m, k, :, HALF:] = second

    def c_terms(g):
        base = at_y(g) * NX

        def step(k, carry):
            start = pl.multiple_of((base + k) * COLS, COLS)
            down[:, pl.ds(start, COLS)] = jnp.dot(
                grads[2], ups[:, pl.ds(start, COLS)], preferred_element_type=F32
            )
            return carry

        lax.fori_loop(0, NX, step, 0)

    def c_own(g, d):
        rows = pl.ds(pl.multiple_of(at_z(d) * 16, 16), 16)
        return down[rows, pl.ds(pl.multiple_of(at_y(g) * NX * COLS, NX * COLS), NX * COLS)]

    class Fold8:
        def __init__(self, k, g, long_way):
            self.k, self.g = k, g
            self.hops = {1: 4 if long_way == 1 else 3, -1: 4 if long_way == -1 else 3}
            self.last = {}

        def hop(self, r):
            for w, way in enumerate((1, -1)):
                if r > self.hops[way]:
                    continue
                value = c_own(self.g, way * (self.hops[way] - r + 1))
                if r > 1:
                    self.last[way].wait_recv()
                    value = value + zgot[w, self.k, r - 2].astype(F32)
                zsent[w, self.k, r - 1] = value.astype(BF16)
                self.last[way] = links.send(
                    zsent.at[w, self.k, r - 1], zgot.at[w, self.k, r - 1], to_z(way)
                )

        def close(self):
            wait_all(self.last.values())
            zpart[self.k] = (
                c_own(self.g, 0)
                + zgot[0, self.k, self.hops[1] - 1].astype(F32)
                + zgot[1, self.k, self.hops[-1] - 1].astype(F32)
            )

    zfolds = [Fold8(k, g, 1 if k % 2 == 0 else -1) for k, g in enumerate(order)]

    def wide_half(d, h):
        return zpart[index[d], :, h * NX * HALF : (h + 1) * NX * HALF]

    c_fold2 = Fold4(wide_half, ysent, ygot, to_y)

    def begin_c(k):
        c_terms(order[k])
        zfolds[k].hop(1)

    now(0)
    begin_c(0)
    now(1)
    begin_c(1)
    begin_c(2)
    relay(0)
    begin_c(3)
    now(2)
    zfolds[0].hop(2)
    relay(1)
    zfolds[1].hop(2)
    now(3)
    zfolds[2].hop(2)
    close(0)
    for fold in folds2:
        fold.far()
    zfolds[3].hop(2)
    relay(2)
    zfolds[0].hop(3)
    close(1)
    for fold in folds2:
        fold.right()
    zfolds[1].hop(3)
    relay(3)
    zfolds[2].hop(3)
    close(2)
    for fold in folds2:
        fold.left()
        fold.relay_right()
        fold.relay_left()
    zfolds[3].hop(3)
    zfolds[0].hop(4)
    zfolds[1].hop(4)
    close(3)

    def last_rows(m):
        first, second = folds2[m].total()
        part1[m, 0, :, :HALF] = first
        part1[m, 0, :, HALF:] = second
        sent3[m] = part1[m, 0].astype(BF16)
        copies = []
        for d in (4, 3, 5, 2, 6, 1, 7):
            rows = pl.ds(pl.multiple_of(at_z(d) * 16, 16), 16)
            copies.append(links.send(sent3.at[m, rows], got3.at[m, d - 1], to_z(d)))
        return copies

    third = [last_rows(0), last_rows(1)]
    zfolds[2].hop(4)
    zfolds[3].hop(4)
    zfolds[0].close()
    c_fold2.far()
    zfolds[1].close()
    c_fold2.right()
    zfolds[2].close()
    c_fold2.left()
    c_fold2.relay_right()
    c_fold2.relay_left()
    zfolds[3].close()
    first, second = c_fold2.total()
    zpart[0, :, : NX * HALF] = first
    zpart[0, :, NX * HALF :] = second
    xsent[...] = zpart[0].astype(BF16)

    def columns(d):
        return pl.ds(pl.multiple_of(at_x(d) * COLS, COLS), COLS)

    c_last = [links.send(xsent.at[:, columns(d)], xgot.at[d - 1], to_x(d)) for d in (2, 1, 3)]
    mine = pl.ds(pl.multiple_of(z * 16, 16), 16)
    for m in range(2):
        wait_all(third[m])
        total = part1[m, 0, mine, :]
        for d in range(NZ - 1):
            total = total + got3[m, d].astype(F32)
        out[m] = total
    wait_all(c_last)
    total = zpart[0, :, columns(0)]
    for d in range(NX - 1):
        total = total + xgot[d].astype(F32)
    out[2] = total
    links.drain()


def on_device(tokens, upstream, weights):
    any_space = pl.BlockSpec(memory_space=pl.ANY)
    vmem = pl.BlockSpec(memory_space=pltpu.VMEM)
    dma = pltpu.SemaphoreType.DMA
    return pl.pallas_call(
        kernel,
        out_shape=jax.ShapeDtypeStruct((3, 16, COLS), F32),
        in_specs=[any_space, any_space, vmem],
        out_specs=vmem,
        scratch_shapes=[
            pltpu.VMEM((2 * TOK, MODEL), BF16),
            pltpu.VMEM((2 * TOK, MODEL), BF16),
            pltpu.VMEM((3, NX * NY, NZ, 64, UNITS), BF16),
            pltpu.VMEM((3, 32, UNITS), BF16),
            pltpu.VMEM((3, UNITS, 2 * TOK), BF16),
            pltpu.VMEM((UNITS, MODEL), F32),
            pltpu.VMEM((2, 4, 6, UNITS, HALF), BF16),
            pltpu.VMEM((2, 4, 6, UNITS, HALF), BF16),
            pltpu.VMEM((2, 4, UNITS, COLS), F32),
            pltpu.VMEM((2, 6, UNITS, HALF), BF16),
            pltpu.VMEM((2, 6, UNITS, HALF), BF16),
            pltpu.VMEM((2, UNITS, COLS), BF16),
            pltpu.VMEM((2, NZ - 1, 16, COLS), BF16),
            pltpu.VMEM((2, 4, 4, 16, NX * COLS), BF16),
            pltpu.VMEM((2, 4, 4, 16, NX * COLS), BF16),
            pltpu.VMEM((4, 16, NX * COLS), F32),
            pltpu.VMEM((6, 16, NX * HALF), BF16),
            pltpu.VMEM((6, 16, NX * HALF), BF16),
            pltpu.VMEM((16, NX * COLS), BF16),
            pltpu.VMEM((NX - 1, 16, COLS), BF16),
            dma((N_COPIES,)),
            dma((N_COPIES,)),
            dma((2,)),
        ],
        compiler_params=pltpu.CompilerParams(
            collective_id=0, has_side_effects=True, vmem_limit_bytes=58 << 20
        ),
        name="bucket_grads",
    )(tokens, upstream, weights)


def solution(mesh):
    placed = (
        P(("outer", "inner"), None),
        P(("outer", "inner"), None),
        P(None, ("outer", "inner"), None),
    )
    return jax.shard_map(
        on_device, mesh=mesh, in_specs=placed, out_specs=P(None, "inner", "outer"), check_vma=False
    )
```

time: 518 us -> 105 us (0.20)
  blocking collectives: 306 us -> 0 us
  waiting for transfers between devices: 128 us -> 0 us
  Pallas kernels: 0 us -> 103 us
  local copies, waits for them, and re-layouts: 34.1 us -> 1.54 us
  other arithmetic: 16.4 us -> 0 us
  matrix products: 15.8 us -> 0 us
  between operations: 13.5 us -> 0.01 us
    all_to_all x3 -> x0, blocking collectives: 306 us -> none  [the longest x2 287 us: exchange_in_pieces(): lax.all_to_all(share, axis, split_axis=0, concat_axis=0, tiled=True)]
    all_gather x1 -> x0, waiting for transfers between devices: 127 us -> none  [on_device(): lax.all_gather(weights, ('outer', 'inner'), axis=1, tiled=True)]
    pallas_call x0 -> x1, Pallas kernels: none -> 103 us  [on_device(): pl.pallas_call(kernel, out_shape=jax.ShapeDtypeStruct((3, 16, COLS), F32)...]
    unnamed x6 -> x1, local copies, waits for them, and re-layouts: 23.6 us -> 1.54 us
    dot_general x6 -> x0, matrix products: 15.8 us -> none  [the longest x1 4.84 us: on_device(): jnp.dot(tokens, full_weights[0], preferred_element_type=jnp.float32)]
    reduce_sum x2 -> x0, other arithmetic: 14.8 us -> none  [combine_received(): return jnp.sum(received.astype(jnp.float32), axis=0)]
    broadcast_in_dim x1 -> x0, local copies, waits for them, and re-layouts: 8.27 us -> none  [on_device(): partial_rounded[None]]
  transfers between devices with their start and end apart: 1 -> 0, of which waited for: 1 -> 0; matrix products, arithmetic and copies ran while one was open for 0% -> 0% of each run, Pallas kernels for 0% -> 0%
where the time goes in v1:
time: 105 us; the launch traced here: 104 us
  Pallas kernels  103 us (98%)
  local copies, waits for them, and re-layouts  1.54 us (1%)
    pallas_call x1, Pallas kernels, on_device(): pl.pallas_call(kernel, out_shape=jax.ShapeDtypeStruct((3, 16, COLS), F32)...  103 us

profile of v1, /device:TPU:32, one launch (start us, length us, event | category | flops | bytes accessed | tf_op | source)
XLA Modules:
  0.0 104.5 jit_solution(380627734630578741)
XLA Ops:
  0.0 102.9 %bucket_grads.1 = f32[3,16,512]{2,1,0:T(8,128)} custom-call(bf16[256,8192]{1,0:T(8,128)(2,1)} %tokens.1, bf16[256,8192]{1,0:T(8,128)(2,1)} %upstream.1, bf16[3,32,256]{2,1,0:T(8,128)(2,1)} %shard.1), custom_call_target="tpu_custom_call" | custom-call | tf_op jit(solution)/shard_map/bucket_grads/pallas_call | solution.py:507
  102.9 1.5 %copy.5 = f32[3,16,512]{2,1,0:T(8,128)} copy(f32[3,16,512]{2,1,0:T(8,128)} %bucket_grads.1) | data formatting | bytes 196608

commit v2 on v1

v2 whole, which is shorter than its diff:
```python
import math

import jax
import jax.numpy as jnp
from jax import lax
from jax.experimental import pallas as pl
from jax.experimental.pallas import tpu as pltpu
from jax.sharding import PartitionSpec as P

MESH = pl.DeviceIdType.MESH
BF16, F32 = jnp.bfloat16, jnp.float32
NX, NY, NZ = 4, 4, 8
COLS = 512
HALF = COLS // 2
UNITS = 128
TOK = 256
MODEL = 8192


def place(x, y, z, c):
    return (y * NX + x, z * 2 + c)


class Links:
    def __init__(self, send_sems, recv_sems, measure):
        self.send_sems, self.recv_sems, self.measure = send_sems, recv_sems, measure
        self.used = 0
        self.sent = [0] * N_SENDS

    def group(self):
        self.used += 1
        return [self.used - 1, 0]

    def send(self, group, src, dst, target, lane=0):
        copy = pltpu.make_async_remote_copy(
            src_ref=src,
            dst_ref=dst,
            send_sem=self.send_sems.at[lane],
            recv_sem=self.recv_sems.at[group[0]],
            device_id=target,
            device_id_type=MESH,
        )
        copy.start()
        size = math.prod(src.shape) * 2
        group[1] += size
        self.sent[lane] += size

    def take(self, sem, size):
        rows, rest = divmod(size, ROW)
        assert rest == 0 and rows <= self.measure.shape[0]
        ref = self.measure.at[pl.ds(0, rows)]
        pltpu.make_async_copy(ref, ref, sem).wait()

    def wait(self, group):
        self.take(self.recv_sems.at[group[0]], group[1])

    def drain(self):
        for lane, size in enumerate(self.sent):
            self.take(self.send_sems.at[lane], size)


N_GROUPS = 88
N_SENDS = 4
SUMS = 3
ROW = 64 * UNITS * 2


def kernel(
    tokens,
    upstream,
    shard_hbm,
    out,
    tok,
    ups,
    full,
    stage,
    shard,
    acc,
    acc3,
    grads,
    down,
    held1,
    sent1,
    got1,
    part1,
    held2,
    sent2,
    got2,
    sent3,
    got3,
    zsent,
    zgot,
    zpart,
    yheld,
    ysent,
    ygot,
    xsent,
    xgot,
    send_sems,
    recv_sems,
    local_sems,
):
    links = Links(send_sems, recv_sems, full.reshape(3 * NX * NY * NZ, 64, UNITS))
    outer, inner = lax.axis_index("outer"), lax.axis_index("inner")
    x, y = lax.rem(outer, NX), lax.div(outer, NX)
    z, c = lax.div(inner, 2), lax.rem(inner, 2)

    def at_x(d):
        return lax.rem(x + d + NX, NX)

    def at_y(d):
        return lax.rem(y + d + NY, NY)

    def at_z(d):
        return lax.rem(z + d + NZ, NZ)

    def to_x(d):
        return place(at_x(d), y, z, c)

    def to_y(d):
        return place(x, at_y(d), z, c)

    def to_z(d):
        return place(x, y, at_z(d), c)

    sibling = place(x, y, z, 1 - c)

    load_tok = pltpu.make_async_copy(tokens, tok.at[pl.ds(0, TOK)], local_sems.at[0])
    load_ups = pltpu.make_async_copy(upstream, ups.at[pl.ds(0, TOK)], local_sems.at[1])
    load_shard = pltpu.make_async_copy(shard_hbm, shard, local_sems.at[2])
    load_shard.start()
    load_tok.start()
    load_ups.start()

    barrier = pltpu.get_barrier_semaphore()
    partners = [sibling]
    partners += [to_x(d) for d in (1, 2, 3)]
    partners += [to_y(d) for d in (1, 3)]
    partners += [to_z(d) for d in range(1, NZ)]
    for partner in partners:
        pl.semaphore_signal(barrier, inc=1, device_id=partner, device_id_type=MESH)

    row = lax.broadcasted_iota(jnp.int32, (256, 256), 0)
    lane = lax.broadcasted_iota(jnp.int32, (256, 256), 1)
    slot = lane % UNITS
    half = jnp.where(lane < UNITS, c, 1 - c)
    pick = (row == (slot // 16) * 32 + half * 16 + slot % 16).astype(F32).astype(BF16)
    home = y * NX + x
    load_shard.wait()
    for m in range(3):
        moved = jnp.dot(shard[m], pick, preferred_element_type=F32).astype(BF16)
        full[m, home, z, pl.ds(pl.multiple_of(c * 32, 32), 32), :] = moved[:, :UNITS]
        stage[m] = moved[:, UNITS:]
    pl.semaphore_wait(barrier, len(partners))

    swap = links.group()
    mine_rows = pl.ds(pl.multiple_of(c * 32, 32), 32)
    swap_copy = pltpu.make_async_remote_copy(
        src_ref=stage,
        dst_ref=full.at[:, home, z, mine_rows],
        send_sem=send_sems.at[N_SENDS],
        recv_sem=recv_sems.at[swap[0]],
        device_id=sibling,
        device_id_type=MESH,
    )
    swap_copy.start()
    swap_copy.wait_recv()
    near = (1, 7, 2, 6, 3, 5, 4)
    block0, block1, block2 = (full.at[m, home, z] for m in range(3))
    a_z, b_z, c_x, tok_in, ups_in = (links.group() for _ in range(5))
    for d in near:
        links.send(a_z, block0, block0, to_z(d))
    for d in (1, 3, 2):
        links.send(c_x, block2, block2, to_x(d))
    for d in near:
        links.send(b_z, block1, block1, to_z(d))
    links.send(tok_in, tokens, tok.at[pl.ds(TOK, TOK)], sibling, 1)
    links.send(ups_in, upstream, ups.at[pl.ds(TOK, TOK)], sibling, 2)

    def plane(yy, zz, x0=0, n=NX):
        return full.at[2, pl.ds(yy * NX + x0, n), zz]

    class Ring4:
        def __init__(self, whole, part, to):
            self.whole, self.part, self.to = whole, part, to

        def first(self):
            self.hop1 = links.group()
            ref = self.whole(0)
            links.send(self.hop1, ref, ref, self.to(1))
            links.send(self.hop1, ref, ref, self.to(-1))

        def forward(self):
            links.wait(self.hop1)
            self.hop2 = links.group()
            right, left = self.part(-1, 0), self.part(1, 1)
            links.send(self.hop2, right, right, self.to(1))
            links.send(self.hop2, left, left, self.to(-1))

        def finish(self):
            links.wait(self.hop2)

    def piece(m, yy, xx, h=None):
        ref = full.at[m, yy * NX + xx]
        return ref if h is None else ref.at[pl.ds(h * 4, 4)]

    a_y = Ring4(lambda d: piece(0, at_y(d), x), lambda d, h: piece(0, at_y(d), x, h), to_y)
    b_x = Ring4(lambda d: piece(1, y, at_x(d)), lambda d, h: piece(1, y, at_x(d), h), to_x)
    c_y = Ring4(lambda d: plane(at_y(d), z), lambda d, h: plane(at_y(d), z, 2 * h, 2), to_y)

    def a_bulk(g):
        return Ring4(
            lambda d: piece(0, at_y(g), at_x(d)), lambda d, h: piece(0, at_y(g), at_x(d), h), to_x
        )

    def b_bulk(g):
        return Ring4(
            lambda d: piece(1, at_y(d), at_x(g)), lambda d, h: piece(1, at_y(d), at_x(g), h), to_y
        )

    class Ring8:
        def __init__(self, g, long_way):
            self.g, self.long_way = g, long_way

        def hop(self, h):
            if h > 1:
                links.wait(self.last)
            self.last = links.group()
            for way in (1, -1) if h < 4 else (self.long_way,):
                ref = plane(at_y(self.g), at_z(-way * (h - 1)))
                links.send(self.last, ref, ref, to_z(way))

        def finish(self):
            links.wait(self.last)

    cz = {g: Ring8(g, 1 if k % 2 == 0 else -1) for k, g in enumerate((0, 1, -1, 2))}
    ax = {g: a_bulk(g) for g in (0, 1, -1, 2)}
    by = {g: b_bulk(g) for g in (0, 1, -1, 2)}

    wait = links.wait
    wait(c_x)
    c_y.first()
    cz[0].hop(1)
    wait(a_z)
    a_y.first()
    ax[0].first()
    c_y.forward()
    cz[1].hop(1)
    cz[-1].hop(1)
    wait(b_z)
    b_x.first()
    by[0].first()
    c_y.finish()
    cz[2].hop(1)
    cz[0].hop(2)
    ax[0].forward()
    a_y.forward()
    ax[1].first()
    cz[1].hop(2)
    cz[-1].hop(2)
    b_x.forward()
    ax[-1].first()
    by[1].first()
    by[-1].first()
    by[0].forward()
    cz[2].hop(2)
    a_y.finish()
    ax[2].first()
    cz[0].hop(3)
    ax[1].forward()
    cz[1].hop(3)
    b_x.finish()
    by[2].first()
    cz[-1].hop(3)
    by[1].forward()
    ax[-1].forward()
    cz[2].hop(3)
    by[-1].forward()
    cz[0].hop(4)
    load_tok.wait()
    load_ups.wait()
    wait(tok_in)

    def group_rows(g):
        return pl.ds(pl.multiple_of(at_y(g) * NX * COLS, NX * COLS), NX * COLS)

    def group_block(m, g):
        return full[m, pl.ds(at_y(g) * NX, NX)].reshape(NX * COLS, UNITS)

    def gate_up(g):
        pair = jnp.concatenate([group_block(0, g), group_block(1, g)], axis=1)
        return jnp.dot(tok[:, group_rows(g)], pair, preferred_element_type=F32)

    def third_product(g):
        return jnp.dot(ups[:, group_rows(g)], group_block(2, g), preferred_element_type=F32)

    ax[0].finish()
    acc[...] = gate_up(0)
    cz[1].hop(4)
    cz[-1].hop(4)
    ax[2].forward()
    by[2].forward()
    cz[2].hop(4)
    ax[1].finish()
    acc[...] += gate_up(1)
    ax[-1].finish()
    acc[...] += gate_up(-1)
    wait(ups_in)
    cz[0].finish()
    acc3[...] = third_product(0)
    cz[1].finish()
    acc3[...] += third_product(1)
    cz[-1].finish()
    acc3[...] += third_product(-1)
    ax[2].finish()
    for g in (0, 1, -1, 2):
        by[g].finish()
    acc[...] += gate_up(2)
    cz[2].finish()
    acc3[...] += third_product(2)
    gate, up, hidden_grad = acc[:, :UNITS], acc[:, UNITS:], acc3[...]
    sigmoid = jax.nn.sigmoid(gate)
    activated = gate * sigmoid
    hidden = activated * up
    grad_gate = hidden_grad * up * sigmoid * (1.0 + gate * (1.0 - sigmoid))
    grad_up = hidden_grad * activated
    grads[2] = hidden.T.astype(BF16)
    grads[0] = grad_gate.T.astype(BF16)
    grads[1] = grad_up.T.astype(BF16)

    def term(m, yy, xx):
        start = pl.multiple_of((yy * NX + xx) * COLS, COLS)
        value = jnp.dot(grads[m], tok[:, pl.ds(start, COLS)], preferred_element_type=F32)
        return value[:, :HALF], value[:, HALF:]

    class Fold4:
        def __init__(self, own, held, sent, got, to):
            self.own, self.held, self.sent, self.got, self.to = own, held, sent, got, to

        def put(self, group, k, value, way):
            self.sent[k] = value.astype(BF16)
            links.send(group, self.sent.at[k], self.got.at[k], self.to(way), SUMS)

        def far(self):
            self.hop1, self.hop2 = links.group(), links.group()
            first, second = self.own(2)
            self.put(self.hop1, 0, first, 1)
            self.put(self.hop1, 1, second, -1)

        def right(self):
            first, second = self.own(1)
            self.put(self.hop2, 2, second, 1)
            self.held[0] = first

        def left(self):
            first, second = self.own(-1)
            self.put(self.hop2, 3, first, -1)
            self.held[1] = second

        def relay(self):
            links.wait(self.hop1)
            self.put(self.hop2, 4, self.held[0] + self.got[0].astype(F32), 1)
            self.put(self.hop2, 5, self.held[1] + self.got[1].astype(F32), -1)

        def total(self):
            links.wait(self.hop2)
            first, second = self.own(0)
            first = first + self.got[4].astype(F32) + self.got[3].astype(F32)
            second = second + self.got[2].astype(F32) + self.got[5].astype(F32)
            return first, second

    order = (2, 1, -1, 0)

    def a_fold(k, g):
        own = lambda d: term(0, at_y(g), at_x(d))
        return Fold4(own, held1.at[0, k], sent1.at[0, k], got1.at[0, k], to_x)

    def b_fold(k, g):
        own = lambda d: term(1, at_y(d), at_x(g))
        return Fold4(own, held1.at[1, k], sent1.at[1, k], got1.at[1, k], to_y)

    fa = [a_fold(k, g) for k, g in enumerate(order)]
    fb = [b_fold(k, g) for k, g in enumerate(order)]
    index = {g: k for k, g in enumerate(order)}

    def halves(m, d):
        return part1[m, index[d], :, :HALF], part1[m, index[d], :, HALF:]

    fa2 = Fold4(lambda d: halves(0, d), held2.at[0], sent2.at[0], got2.at[0], to_y)
    fb2 = Fold4(lambda d: halves(1, d), held2.at[1], sent2.at[1], got2.at[1], to_x)

    def close(m, k):
        first, second = (fa, fb)[m][k].total()
        part1[m, k, :, :HALF] = first
        part1[m, k, :, HALF:] = second

    def c_terms(g):
        base = at_y(g) * NX

        def step(k, carry):
            start = pl.multiple_of((base + k) * COLS, COLS)
            down[:, pl.ds(start, COLS)] = jnp.dot(
                grads[2], ups[:, pl.ds(start, COLS)], preferred_element_type=F32
            )
            return carry

        lax.fori_loop(0, NX, step, 0)

    def c_own(g, d):
        rows = pl.ds(pl.multiple_of(at_z(d) * 16, 16), 16)
        return down[rows, pl.ds(pl.multiple_of(at_y(g) * NX * COLS, NX * COLS), NX * COLS)]

    class Fold8:
        def __init__(self, k, g, long_way):
            self.k, self.g = k, g
            self.hops = {1: 4 if long_way == 1 else 3, -1: 4 if long_way == -1 else 3}

        def hop(self, r):
            if r > 1:
                links.wait(self.last)
            self.last = links.group()
            for w, way in enumerate((1, -1)):
                if r > self.hops[way]:
                    continue
                value = c_own(self.g, way * (self.hops[way] - r + 1))
                if r > 1:
                    value = value + zgot[w, self.k, r - 2].astype(F32)
                zsent[w, self.k, r - 1] = value.astype(BF16)
                links.send(
                    self.last, zsent.at[w, self.k, r - 1], zgot.at[w, self.k, r - 1], to_z(way), SUMS
                )

        def close(self):
            links.wait(self.last)
            zpart[self.k] = (
                c_own(self.g, 0)
                + zgot[0, self.k, self.hops[1] - 1].astype(F32)
                + zgot[1, self.k, self.hops[-1] - 1].astype(F32)
            )

    zf = [Fold8(k, g, 1 if k % 2 == 0 else -1) for k, g in enumerate(order)]

    def wide_halves(d):
        return zpart[index[d], :, : NX * HALF], zpart[index[d], :, NX * HALF :]

    fc2 = Fold4(wide_halves, yheld, ysent, ygot, to_y)

    def begin_c(k):
        c_terms(order[k])
        zf[k].hop(1)

    def spread(m):
        first, second = (fa2, fb2)[m].total()
        part1[m, 0, :, :HALF] = first
        part1[m, 0, :, HALF:] = second
        sent3[m] = part1[m, 0].astype(BF16)
        group = links.group()
        for d in (4, 3, 5, 2, 6, 1, 7):
            rows = pl.ds(pl.multiple_of(at_z(d) * 16, 16), 16)
            links.send(group, sent3.at[m, rows], got3.at[m, d - 1], to_z(d), SUMS)
        return group

    begin_c(0)
    fa[0].far()
    fb[0].far()
    begin_c(1)
    fa[0].right()
    fa[0].left()
    fb[0].right()
    fb[0].left()
    begin_c(2)
    zf[0].hop(2)
    fa[0].relay()
    fa[1].far()
    fb[0].relay()
    fb[1].far()
    begin_c(3)
    zf[1].hop(2)
    fa[1].right()
    fa[1].left()
    fb[1].right()
    fb[1].left()
    zf[2].hop(2)
    fa[1].relay()
    fa[2].far()
    fb[1].relay()
    fb[2].far()
    zf[3].hop(2)
    fa[2].right()
    fa[2].left()
    fb[2].right()
    fb[2].left()
    zf[0].hop(3)
    close(0, 0)
    fa2.far()
    close(1, 0)
    fb2.far()
    fa[2].relay()
    fa[3].far()
    fb[2].relay()
    fb[3].far()
    zf[1].hop(3)
    fa[3].right()
    fa[3].left()
    fb[3].right()
    fb[3].left()
    zf[2].hop(3)
    close(0, 1)
    fa2.right()
    close(1, 1)
    fb2.right()
    zf[3].hop(3)
    fa[3].relay()
    fb[3].relay()
    zf[0].hop(4)
    close(0, 2)
    fa2.left()
    fa2.relay()
    close(1, 2)
    fb2.left()
    fb2.relay()
    zf[1].hop(4)
    zf[2].hop(4)
    zf[3].hop(4)
    close(0, 3)
    third0 = spread(0)
    close(1, 3)
    third1 = spread(1)
    zf[0].close()
    fc2.far()
    zf[1].close()
    fc2.right()
    zf[2].close()
    fc2.left()
    fc2.relay()
    zf[3].close()
    first, second = fc2.total()
    zpart[0, :, : NX * HALF] = first
    zpart[0, :, NX * HALF :] = second
    xsent[...] = zpart[0].astype(BF16)

    def columns(d):
        return pl.ds(pl.multiple_of(at_x(d) * COLS, COLS), COLS)

    last = links.group()
    for d in (2, 1, 3):
        links.send(last, xsent.at[:, columns(d)], xgot.at[d - 1], to_x(d), SUMS)
    mine = pl.ds(pl.multiple_of(z * 16, 16), 16)
    for m, group in enumerate((third0, third1)):
        wait(group)
        total = part1[m, 0, mine, :]
        for d in range(NZ - 1):
            total = total + got3[m, d].astype(F32)
        out[m] = total
    wait(last)
    total = zpart[0, :, columns(0)]
    for d in range(NX - 1):
        total = total + xgot[d].astype(F32)
    out[2] = total
    links.drain()
    swap_copy.wait_send()
    assert links.used <= N_GROUPS


def on_device(tokens, upstream, weights):
    any_space = pl.BlockSpec(memory_space=pl.ANY)
    vmem = pl.BlockSpec(memory_space=pltpu.VMEM)
    dma = pltpu.SemaphoreType.DMA
    return pl.pallas_call(
        kernel,
        out_shape=jax.ShapeDtypeStruct((3, 16, COLS), F32),
        in_specs=[any_space, any_space, any_space],
        out_specs=vmem,
        scratch_shapes=[
            pltpu.VMEM((2 * TOK, MODEL), BF16),
            pltpu.VMEM((2 * TOK, MODEL), BF16),
            pltpu.VMEM((3, NX * NY, NZ, 64, UNITS), BF16),
            pltpu.VMEM((3, 32, UNITS), BF16),
            pltpu.VMEM((3, 32, 2 * UNITS), BF16),
            pltpu.VMEM((2 * TOK, 2 * UNITS), F32),
            pltpu.VMEM((2 * TOK, UNITS), F32),
            pltpu.VMEM((3, UNITS, 2 * TOK), BF16),
            pltpu.VMEM((UNITS, MODEL), F32),
            pltpu.VMEM((2, 4, 2, UNITS, HALF), F32),
            pltpu.VMEM((2, 4, 6, UNITS, HALF), BF16),
            pltpu.VMEM((2, 4, 6, UNITS, HALF), BF16),
            pltpu.VMEM((2, 4, UNITS, COLS), F32),
            pltpu.VMEM((2, 2, UNITS, HALF), F32),
            pltpu.VMEM((2, 6, UNITS, HALF), BF16),
            pltpu.VMEM((2, 6, UNITS, HALF), BF16),
            pltpu.VMEM((2, UNITS, COLS), BF16),
            pltpu.VMEM((2, NZ - 1, 16, COLS), BF16),
            pltpu.VMEM((2, 4, 4, 16, NX * COLS), BF16),
            pltpu.VMEM((2, 4, 4, 16, NX * COLS), BF16),
            pltpu.VMEM((4, 16, NX * COLS), F32),
            pltpu.VMEM((2, 16, NX * HALF), F32),
            pltpu.VMEM((6, 16, NX * HALF), BF16),
            pltpu.VMEM((6, 16, NX * HALF), BF16),
            pltpu.VMEM((16, NX * COLS), BF16),
            pltpu.VMEM((NX - 1, 16, COLS), BF16),
            dma((N_SENDS + 1,)),
            dma((N_GROUPS,)),
            dma((3,)),
        ],
        compiler_params=pltpu.CompilerParams(
            collective_id=0, has_side_effects=True, vmem_limit_bytes=58 << 20
        ),
        name="bucket_grads",
    )(tokens, upstream, weights)


def solution(mesh):
    placed = (
        P(("outer", "inner"), None),
        P(("outer", "inner"), None),
        P(None, ("outer", "inner"), None),
    )
    return jax.shard_map(
        on_device, mesh=mesh, in_specs=placed, out_specs=P(None, "inner", "outer"), check_vma=False
    )
```

time: 105 us -> 87.7 us (0.84)
  Pallas kernels: 103 us -> 85.2 us
    pallas_call x1, Pallas kernels: 103 us -> 85.2 us  [on_device(): pl.pallas_call(kernel, out_shape=jax.ShapeDtypeStruct((3, 16, COLS), F32)...]
where the time goes in v2:
time: 87.7 us; the launch traced here: 86.7 us
  Pallas kernels  85.2 us (97%)
  local copies, waits for them, and re-layouts  1.54 us (2%)
    pallas_call x1, Pallas kernels, on_device(): pl.pallas_call(kernel, out_shape=jax.ShapeDtypeStruct((3, 16, COLS), F32)...  85.2 us

profile of v2, /device:TPU:32, one launch (start us, length us, event | category | flops | bytes accessed | tf_op | source)
XLA Modules:
  0.0 86.7 jit_solution(611781962928157673)
XLA Ops:
  0.0 85.2 %bucket_grads.1 = f32[3,16,512]{2,1,0:T(8,128)} custom-call(bf16[256,8192]{1,0:T(8,128)(2,1)} %tokens.1, bf16[256,8192]{1,0:T(8,128)(2,1)} %upstream.1, bf16[3,32,256]{2,1,0:T(8,128)(2,1)} %shard_hbm.1), custom_call_target="tpu_custom_call" | custom-call | tf_op jit(solution)/shard_map/bucket_grads/pallas_call | solution.py:569
  85.2 1.5 %copy.5 = f32[3,16,512]{2,1,0:T(8,128)} copy(f32[3,16,512]{2,1,0:T(8,128)} %bucket_grads.1) | data formatting | bytes 196608

commit v3 on v2

v3 whole, which is shorter than its diff:
```python
import functools
import math

import jax
import jax.numpy as jnp
from jax import lax
from jax.experimental import pallas as pl
from jax.experimental.pallas import tpu as pltpu
from jax.sharding import PartitionSpec as P

MESH = pl.DeviceIdType.MESH
BF16, F32 = jnp.bfloat16, jnp.float32
NX, NY, NZ = 4, 4, 8
COLS = 512
HALF = COLS // 2
UNITS = 128
TOK = 256
MODEL = 8192


def place(x, y, z, c):
    return (y * NX + x, z * 2 + c)


ORDER = (
    0, 11, 1, 3, 7, 2, 27, 19,
    9, 5, 40, 12, 4, 23, 8, 15,
    35, 28, 20, 6, 42, 17, 41, 10,
    45, 13, 50, 25, 31, 36, 24, 29,
    18, 51, 21, 55, 14, 16, 46, 37,
    33, 43, 26, 47, 30, 52, 22, 32,
    56, 39, 34, 53, 38, 44, 48, 57,
    49, 58, 59, 113, 118, 119, 115, 54,
    60, 87, 61, 88, 76, 92, 94, 93,
    66, 62, 89, 114, 120, 95, 121, 90,
    77, 71, 67, 116, 123, 124, 125, 63,
    97, 99, 78, 98, 122, 91, 107, 117,
    72, 133, 134, 126, 100, 68, 128, 130,
    64, 129, 102, 103, 104, 79, 96, 108,
    127, 135, 136, 73, 131, 101, 109, 110,
    69, 105, 80, 65, 81, 74, 132, 137,
    70, 82, 106, 75, 83, 111, 84, 138,
    85, 86, 112,
)


class Links:
    def __init__(self, send_sems, recv_sems, measure):
        self.send_sems, self.recv_sems, self.measure = send_sems, recv_sems, measure
        self.used = 0
        self.sent = [0] * N_SENDS

    def group(self):
        self.used += 1
        return [self.used - 1, 0, False]

    def send(self, group, src, dst, target, lane=0):
        copy = pltpu.make_async_remote_copy(
            src_ref=src,
            dst_ref=dst,
            send_sem=self.send_sems.at[lane],
            recv_sem=self.recv_sems.at[group[0]],
            device_id=target,
            device_id_type=MESH,
        )
        copy.start()
        size = math.prod(src.shape) * 2
        group[1] += size
        self.sent[lane] += size

    def take(self, sem, size):
        rows, rest = divmod(size, ROW)
        assert rest == 0 and rows <= self.measure.shape[0]
        ref = self.measure.at[pl.ds(0, rows)]
        pltpu.make_async_copy(ref, ref, sem).wait()

    def wait(self, group):
        if not group[2]:
            group[2] = True
            self.take(self.recv_sems.at[group[0]], group[1])

    def drain(self):
        for lane, size in enumerate(self.sent):
            self.take(self.send_sems.at[lane], size)


ROLES = ("z", "yx", "xy")
N_GROUPS = 88
N_SENDS = 4
SUMS = 3
ROW = 64 * UNITS * 2


def kernel(
    tokens,
    upstream,
    shard_hbm,
    out,
    tok,
    ups,
    full,
    stage,
    shard,
    acc,
    acc3,
    grads,
    factors,
    zterms,
    held1,
    sent1,
    got1,
    part1,
    held2,
    sent2,
    got2,
    last1,
    sent3,
    got3,
    zsent,
    zgot,
    zpart,
    yheld,
    ysent,
    ygot,
    last2,
    xsent,
    xgot,
    send_sems,
    recv_sems,
    local_sems,
):
    links = Links(send_sems, recv_sems, full.reshape(3 * NX * NY * NZ, 64, UNITS))
    outer, inner = lax.axis_index("outer"), lax.axis_index("inner")
    x, y = lax.rem(outer, NX), lax.div(outer, NX)
    z, c = lax.div(inner, 2), lax.rem(inner, 2)

    def at_x(d):
        return lax.rem(x + d + NX, NX)

    def at_y(d):
        return lax.rem(y + d + NY, NY)

    def at_z(d):
        return lax.rem(z + d + NZ, NZ)

    def to_x(d):
        return place(at_x(d), y, z, c)

    def to_y(d):
        return place(x, at_y(d), z, c)

    def to_z(d):
        return place(x, y, at_z(d), c)

    sibling = place(x, y, z, 1 - c)

    load_tok = pltpu.make_async_copy(tokens, tok.at[pl.ds(0, TOK)], local_sems.at[0])
    load_ups = pltpu.make_async_copy(upstream, ups.at[pl.ds(0, TOK)], local_sems.at[1])
    load_shard = pltpu.make_async_copy(shard_hbm, shard, local_sems.at[2])
    load_shard.start()
    load_tok.start()
    load_ups.start()

    barrier = pltpu.get_barrier_semaphore()
    partners = [sibling]
    partners += [to_x(d) for d in (1, 2, 3)]
    partners += [to_y(d) for d in (1, 3)]
    partners += [to_z(d) for d in range(1, NZ)]
    for partner in partners:
        pl.semaphore_signal(barrier, inc=1, device_id=partner, device_id_type=MESH)

    row = lax.broadcasted_iota(jnp.int32, (256, 256), 0)
    lane = lax.broadcasted_iota(jnp.int32, (256, 256), 1)
    slot = lane % UNITS
    half = jnp.where(lane < UNITS, c, 1 - c)
    pick = (row == (slot // 16) * 32 + half * 16 + slot % 16).astype(F32).astype(BF16)
    home = y * NX + x
    load_shard.wait()
    for m in range(3):
        moved = jnp.dot(shard[m], pick, preferred_element_type=F32).astype(BF16)
        full[m, home, z, pl.ds(pl.multiple_of(c * 32, 32), 32), :] = moved[:, :UNITS]
        stage[m] = moved[:, UNITS:]
    pl.semaphore_wait(barrier, len(partners))

    swap = links.group()
    mine_rows = pl.ds(pl.multiple_of(c * 32, 32), 32)
    swap_copy = pltpu.make_async_remote_copy(
        src_ref=stage,
        dst_ref=full.at[:, home, z, mine_rows],
        send_sem=send_sems.at[N_SENDS],
        recv_sem=recv_sems.at[swap[0]],
        device_id=sibling,
        device_id_type=MESH,
    )
    swap_copy.start()
    swap_copy.wait_recv()
    near = (1, 7, 2, 6, 3, 5, 4)
    block0, block1, block2 = (full.at[m, home, z] for m in range(3))
    a_z, b_z, c_x, tok_in, ups_in = (links.group() for _ in range(5))
    for d in near:
        links.send(a_z, block0, block0, to_z(d))
    for d in (1, 3, 2):
        links.send(c_x, block2, block2, to_x(d))
    for d in near:
        links.send(b_z, block1, block1, to_z(d))
    links.send(tok_in, tokens, tok.at[pl.ds(TOK, TOK)], sibling, 1)
    links.send(ups_in, upstream, ups.at[pl.ds(TOK, TOK)], sibling, 2)

    def plane(yy, zz, x0=0, n=NX):
        return full.at[2, pl.ds(yy * NX + x0, n), zz]

    class Ring4:
        def __init__(self, whole, part, to, ready):
            self.whole, self.part, self.to, self.ready = whole, part, to, ready

        def first(self):
            for group in self.ready():
                links.wait(group)
            self.hop1 = links.group()
            ref = self.whole(0)
            links.send(self.hop1, ref, ref, self.to(1))
            links.send(self.hop1, ref, ref, self.to(-1))

        def forward(self):
            links.wait(self.hop1)
            self.hop2 = links.group()
            right, left = self.part(-1, 0), self.part(1, 1)
            links.send(self.hop2, right, right, self.to(1))
            links.send(self.hop2, left, left, self.to(-1))

        def finish(self):
            links.wait(self.hop2)

    def piece(m, yy, xx, h=None):
        ref = full.at[m, yy * NX + xx]
        return ref if h is None else ref.at[pl.ds(h * 4, 4)]

    a_y = Ring4(
        lambda d: piece(0, at_y(d), x), lambda d, h: piece(0, at_y(d), x, h), to_y, lambda: (a_z,)
    )
    b_x = Ring4(
        lambda d: piece(1, y, at_x(d)), lambda d, h: piece(1, y, at_x(d), h), to_x, lambda: (b_z,)
    )
    c_y = Ring4(
        lambda d: plane(at_y(d), z), lambda d, h: plane(at_y(d), z, 2 * h, 2), to_y, lambda: (c_x,)
    )

    def whole_block(start, ring, g):
        return (start,) if g == 0 else (ring.hop2,) if g == 2 else (ring.hop1,)

    def a_bulk(g):
        return Ring4(
            lambda d: piece(0, at_y(g), at_x(d)),
            lambda d, h: piece(0, at_y(g), at_x(d), h),
            to_x,
            lambda: whole_block(a_z, a_y, g),
        )

    def b_bulk(g):
        return Ring4(
            lambda d: piece(1, at_y(d), at_x(g)),
            lambda d, h: piece(1, at_y(d), at_x(g), h),
            to_y,
            lambda: whole_block(b_z, b_x, g),
        )

    class Ring8:
        def __init__(self, g, long_way):
            self.g, self.long_way = g, long_way

        def hop(self, h):
            for group in (self.last,) if h > 1 else whole_block(c_x, c_y, self.g):
                links.wait(group)
            self.last = links.group()
            for way in (1, -1) if h < 4 else (self.long_way,):
                ref = plane(at_y(self.g), at_z(-way * (h - 1)))
                links.send(self.last, ref, ref, to_z(way))

        def finish(self):
            links.wait(self.last)

    cz = {g: Ring8(g, 1 if k % 2 == 0 else -1) for k, g in enumerate((0, 1, -1, 2))}
    ax = {g: a_bulk(g) for g in (0, 1, -1, 2)}
    by = {g: b_bulk(g) for g in (0, 1, -1, 2)}

    wait = links.wait
    steps = [lambda: None]
    for ring in (c_y, a_y, b_x):
        steps += [ring.first, ring.forward]
    for g in (0, 1, -1, 2):
        for ring in (ax[g], by[g]):
            steps += [ring.first, ring.forward]
        steps += [functools.partial(cz[g].hop, h) for h in (1, 2, 3, 4)]

    done = set()

    def once(key, action):
        if key not in done:
            done.add(key)
            action()

    def gate_up(dy, dx):
        once("tok", load_tok.wait)
        wait(tok_in)
        at0 = ax[dy].hop2 if dx == 2 else ax[dy].hop1 if dx else whole_block(a_z, a_y, dy)[0]
        at1 = by[dx].hop2 if dy == 2 else by[dx].hop1 if dy else whole_block(b_z, b_x, dx)[0]
        wait(at0)
        wait(at1)
        k = at_y(dy) * NX + at_x(dx)
        pair = jnp.concatenate([full[m, k].reshape(COLS, UNITS) for m in range(2)], axis=1)
        rows = pl.ds(pl.multiple_of(k * COLS, COLS), COLS)
        value = jnp.dot(tok[:, rows], pair, preferred_element_type=F32)
        if "gate_up" in done:
            acc[...] += value
        else:
            acc[...] = value
        done.add("gate_up")

    def third_product(g):
        once("ups", load_ups.wait)
        wait(ups_in)
        cz[g].finish()
        rows = pl.ds(pl.multiple_of(at_y(g) * NX * COLS, NX * COLS), NX * COLS)
        block = full[2, pl.ds(at_y(g) * NX, NX)].reshape(NX * COLS, UNITS)
        value = jnp.dot(ups[:, rows], block, preferred_element_type=F32)
        if "third" in done:
            acc3[...] += value
        else:
            acc3[...] = value
        done.add("third")

    def activate():
        gate, up = acc[:, :UNITS], acc[:, UNITS:]
        sigmoid = jax.nn.sigmoid(gate)
        activated = gate * sigmoid
        grads[2] = (activated * up).astype(BF16).T
        factors[1] = activated
        factors[0] = up * sigmoid * (1.0 + gate * (1.0 - sigmoid))

    def differentiate():
        hidden_grad = acc3[...]
        for m in range(2):
            grads[m] = (hidden_grad * factors[m]).astype(BF16).T

    for dy in (0, 1, -1, 2):
        steps.append(functools.partial(third_product, dy))
        steps += [functools.partial(gate_up, dy, dx) for dx in (0, 1, -1, 2)]
    steps += [activate, differentiate]

    def term(m, yy, xx):
        start = pl.multiple_of((yy * NX + xx) * COLS, COLS)
        source = ups if m == 2 else tok
        value = jnp.dot(grads[m], source[:, pl.ds(start, COLS)], preferred_element_type=F32)
        return value[:, :HALF], value[:, HALF:]

    class Fold4:
        def __init__(self, own, held, sent, got, to):
            self.own, self.held, self.sent, self.got, self.to = own, held, sent, got, to

        def steps(self):
            return [self.far, self.right, self.left, self.relay]

        def put(self, group, k, value, way):
            self.sent[k] = value.astype(BF16)
            links.send(group, self.sent.at[k], self.got.at[k], self.to(way), SUMS)

        def far(self):
            self.hop1, self.hop2 = links.group(), links.group()
            first, second = self.own(2)
            self.put(self.hop1, 0, first, 1)
            self.put(self.hop1, 1, second, -1)

        def right(self):
            first, second = self.own(1)
            self.put(self.hop2, 2, second, 1)
            self.held[0] = first

        def left(self):
            first, second = self.own(-1)
            self.put(self.hop2, 3, first, -1)
            self.held[1] = second

        def relay(self):
            links.wait(self.hop1)
            self.put(self.hop2, 4, self.held[0] + self.got[0].astype(F32), 1)
            self.put(self.hop2, 5, self.held[1] + self.got[1].astype(F32), -1)

        def total(self):
            links.wait(self.hop2)
            first, second = self.own(0)
            first = first + self.got[4].astype(F32) + self.got[3].astype(F32)
            second = second + self.got[2].astype(F32) + self.got[5].astype(F32)
            return first, second

    order = (2, 1, -1, 0)
    index = {g: k for k, g in enumerate(order)}
    mine = pl.ds(pl.multiple_of(z * 16, 16), 16)

    class Sums:
        def __init__(self, slot, m, x_first):
            self.m, self.slot = m, slot
            to1, to2 = (to_x, to_y) if x_first else (to_y, to_x)

            def own(g, d):
                return term(m, at_y(g), at_x(d)) if x_first else term(m, at_y(d), at_x(g))

            self.folds = [
                Fold4(
                    functools.partial(own, g),
                    held1.at[slot, k],
                    sent1.at[slot, k],
                    got1.at[slot, k],
                    to1,
                )
                for k, g in enumerate(order)
            ]
            self.second = Fold4(self.halves, held2.at[slot], sent2.at[slot], got2.at[slot], to2)
            self.steps = []
            for k, fold in enumerate(self.folds):
                self.steps += fold.steps() + [functools.partial(self.close, k)]
            self.steps += self.second.steps() + [self.spread, self.out]

        def halves(self, d):
            k = index[d]
            return part1[self.slot, k, :, :HALF], part1[self.slot, k, :, HALF:]

        def close(self, k):
            first, second = self.folds[k].total()
            part1[self.slot, k, :, :HALF] = first
            part1[self.slot, k, :, HALF:] = second

        def spread(self):
            slot = self.slot
            first, second = self.second.total()
            last1[slot, :, :HALF] = first
            last1[slot, :, HALF:] = second
            sent3[slot] = last1[slot].astype(BF16)
            self.last = links.group()
            for d in (4, 3, 5, 2, 6, 1, 7):
                rows = pl.ds(pl.multiple_of(at_z(d) * 16, 16), 16)
                links.send(self.last, sent3.at[slot, rows], got3.at[slot, d - 1], to_z(d), SUMS)

        def out(self):
            wait(self.last)
            total = last1[self.slot, mine, :]
            for d in range(NZ - 1):
                total = total + got3[self.slot, d].astype(F32)
            out[self.m] = total

    class Fold8:
        def __init__(self, m, k, g, long_way):
            self.m, self.k, self.g = m, k, g
            self.hops = {1: 4 if long_way == 1 else 3, -1: 4 if long_way == -1 else 3}

        def terms(self):
            source, base = (ups if self.m == 2 else tok), at_y(self.g) * NX

            def step(k, carry):
                start = pl.multiple_of((base + k) * COLS, COLS)
                zterms[:, pl.ds(start, COLS)] = jnp.dot(
                    grads[self.m], source[:, pl.ds(start, COLS)], preferred_element_type=F32
                )
                return carry

            lax.fori_loop(0, NX, step, 0)

        def own(self, d):
            rows = pl.ds(pl.multiple_of(at_z(d) * 16, 16), 16)
            width = NX * COLS
            return zterms[rows, pl.ds(pl.multiple_of(at_y(self.g) * width, width), width)]

        def hop(self, r):
            if r == 1:
                self.terms()
            else:
                wait(self.last)
            self.last = links.group()
            for w, way in enumerate((1, -1)):
                if r > self.hops[way]:
                    continue
                value = self.own(way * (self.hops[way] - r + 1))
                if r > 1:
                    value = value + zgot[w, self.k, r - 2].astype(F32)
                zsent[w, self.k, r - 1] = value.astype(BF16)
                links.send(
                    self.last, zsent.at[w, self.k, r - 1], zgot.at[w, self.k, r - 1], to_z(way), SUMS
                )

        def close(self):
            wait(self.last)
            zpart[self.k] = (
                self.own(0)
                + zgot[0, self.k, self.hops[1] - 1].astype(F32)
                + zgot[1, self.k, self.hops[-1] - 1].astype(F32)
            )

    class ZSums:
        def __init__(self, m):
            self.m = m
            self.folds = [Fold8(m, k, g, 1 if k % 2 == 0 else -1) for k, g in enumerate(order)]
            self.second = Fold4(self.halves, yheld, ysent, ygot, to_y)
            self.steps = []
            for fold in self.folds:
                self.steps += [functools.partial(fold.hop, r) for r in (1, 2, 3, 4)] + [fold.close]
            self.steps += self.second.steps() + [self.spread, self.out]

        def halves(self, d):
            return zpart[index[d], :, : NX * HALF], zpart[index[d], :, NX * HALF :]

        def columns(self, d):
            return pl.ds(pl.multiple_of(at_x(d) * COLS, COLS), COLS)

        def spread(self):
            first, second = self.second.total()
            last2[:, : NX * HALF] = first
            last2[:, NX * HALF :] = second
            xsent[...] = last2[...].astype(BF16)
            self.last = links.group()
            for d in (2, 1, 3):
                links.send(self.last, xsent.at[:, self.columns(d)], xgot.at[d - 1], to_x(d), SUMS)

        def out(self):
            wait(self.last)
            total = last2[:, self.columns(0)]
            for d in range(NX - 1):
                total = total + xgot[d].astype(F32)
            out[self.m] = total

    slot = 0
    for m in range(3):
        if ROLES[m] == "z":
            steps += ZSums(m).steps
        else:
            steps += Sums(slot, m, ROLES[m] == "xy").steps
            slot += 1

    assert sorted(ORDER) == list(range(len(steps)))
    for number in ORDER:
        steps[number]()
    links.drain()
    swap_copy.wait_send()
    assert links.used <= N_GROUPS


def on_device(tokens, upstream, weights):
    any_space = pl.BlockSpec(memory_space=pl.ANY)
    vmem = pl.BlockSpec(memory_space=pltpu.VMEM)
    dma = pltpu.SemaphoreType.DMA
    return pl.pallas_call(
        kernel,
        out_shape=jax.ShapeDtypeStruct((3, 16, COLS), F32),
        in_specs=[any_space, any_space, any_space],
        out_specs=vmem,
        scratch_shapes=[
            pltpu.VMEM((2 * TOK, MODEL), BF16),
            pltpu.VMEM((2 * TOK, MODEL), BF16),
            pltpu.VMEM((3, NX * NY, NZ, 64, UNITS), BF16),
            pltpu.VMEM((3, 32, UNITS), BF16),
            pltpu.VMEM((3, 32, 2 * UNITS), BF16),
            pltpu.VMEM((2 * TOK, 2 * UNITS), F32),
            pltpu.VMEM((2 * TOK, UNITS), F32),
            pltpu.VMEM((3, UNITS, 2 * TOK), BF16),
            pltpu.VMEM((2, 2 * TOK, UNITS), F32),
            pltpu.VMEM((UNITS, MODEL), F32),
            pltpu.VMEM((2, 4, 2, UNITS, HALF), F32),
            pltpu.VMEM((2, 4, 6, UNITS, HALF), BF16),
            pltpu.VMEM((2, 4, 6, UNITS, HALF), BF16),
            pltpu.VMEM((2, 4, UNITS, COLS), F32),
            pltpu.VMEM((2, 2, UNITS, HALF), F32),
            pltpu.VMEM((2, 6, UNITS, HALF), BF16),
            pltpu.VMEM((2, 6, UNITS, HALF), BF16),
            pltpu.VMEM((2, UNITS, COLS), F32),
            pltpu.VMEM((2, UNITS, COLS), BF16),
            pltpu.VMEM((2, NZ - 1, 16, COLS), BF16),
            pltpu.VMEM((2, 4, 4, 16, NX * COLS), BF16),
            pltpu.VMEM((2, 4, 4, 16, NX * COLS), BF16),
            pltpu.VMEM((4, 16, NX * COLS), F32),
            pltpu.VMEM((2, 16, NX * HALF), F32),
            pltpu.VMEM((6, 16, NX * HALF), BF16),
            pltpu.VMEM((6, 16, NX * HALF), BF16),
            pltpu.VMEM((16, NX * COLS), F32),
            pltpu.VMEM((16, NX * COLS), BF16),
            pltpu.VMEM((NX - 1, 16, COLS), BF16),
            dma((N_SENDS + 1,)),
            dma((N_GROUPS,)),
            dma((3,)),
        ],
        compiler_params=pltpu.CompilerParams(
            collective_id=0, has_side_effects=True, vmem_limit_bytes=58 << 20
        ),
        name="bucket_grads",
    )(tokens, upstream, weights)


def solution(mesh):
    placed = (
        P(("outer", "inner"), None),
        P(("outer", "inner"), None),
        P(None, ("outer", "inner"), None),
    )
    return jax.shard_map(
        on_device, mesh=mesh, in_specs=placed, out_specs=P(None, "inner", "outer"), check_vma=False
    )
```

time: 87.7 us -> 83.5 us (0.952)
  Pallas kernels: 85.2 us -> 81 us
    pallas_call x1, Pallas kernels: 85.2 us -> 81 us  [on_device(): pl.pallas_call(kernel, out_shape=jax.ShapeDtypeStruct((3, 16, COLS), F32)...]
where the time goes in v3:
time: 83.5 us; the launch traced here: 82.5 us
  Pallas kernels  81 us (97%)
  local copies, waits for them, and re-layouts  1.54 us (2%)
    pallas_call x1, Pallas kernels, on_device(): pl.pallas_call(kernel, out_shape=jax.ShapeDtypeStruct((3, 16, COLS), F32)...  81 us

profile of v3, /device:TPU:32, one launch (start us, length us, event | category | flops | bytes accessed | tf_op | source)
XLA Modules:
  0.0 82.5 jit_solution(9574839710734226348)
XLA Ops:
  0.0 81.0 %bucket_grads.1 = f32[3,16,512]{2,1,0:T(8,128)} custom-call(bf16[256,8192]{1,0:T(8,128)(2,1)} %tokens.1, bf16[256,8192]{1,0:T(8,128)(2,1)} %upstream.1, bf16[3,32,256]{2,1,0:T(8,128)(2,1)} %shard_hbm.1), custom_call_target="tpu_custom_call" | custom-call | tf_op jit(solution)/shard_map/bucket_grads/pallas_call | solution.py:549
  81.0 1.5 %copy.5 = f32[3,16,512]{2,1,0:T(8,128)} copy(f32[3,16,512]{2,1,0:T(8,128)} %bucket_grads.1) | data formatting | bytes 196608

commit v4 on v3

--- a/solution.py
+++ b/solution.py
@@ -23,24 +23,24 @@
 
 
 ORDER = (
-    0, 11, 1, 3, 7, 2, 27, 19,
-    9, 5, 40, 12, 4, 23, 8, 15,
-    35, 28, 20, 6, 42, 17, 41, 10,
-    45, 13, 50, 25, 31, 36, 24, 29,
-    18, 51, 21, 55, 14, 16, 46, 37,
-    33, 43, 26, 47, 30, 52, 22, 32,
-    56, 39, 34, 53, 38, 44, 48, 57,
-    49, 58, 59, 113, 118, 119, 115, 54,
-    60, 87, 61, 88, 76, 92, 94, 93,
-    66, 62, 89, 114, 120, 95, 121, 90,
-    77, 71, 67, 116, 123, 124, 125, 63,
-    97, 99, 78, 98, 122, 91, 107, 117,
-    72, 133, 134, 126, 100, 68, 128, 130,
-    64, 129, 102, 103, 104, 79, 96, 108,
-    127, 135, 136, 73, 131, 101, 109, 110,
-    69, 105, 80, 65, 81, 74, 132, 137,
-    70, 82, 106, 75, 83, 111, 84, 138,
-    85, 86, 112,
+    0, 1, 11, 3, 7, 5, 9, 2,
+    27, 19, 12, 40, 8, 4, 23, 15,
+    28, 6, 17, 41, 10, 45, 35, 42,
+    25, 13, 20, 50, 31, 29, 24, 36,
+    51, 18, 14, 55, 46, 16, 21, 33,
+    43, 30, 26, 52, 47, 37, 56, 32,
+    39, 22, 34, 53, 48, 49, 57, 38,
+    44, 58, 59, 123, 124, 118, 119, 120,
+    54, 60, 76, 87, 89, 88, 92, 61,
+    121, 102, 66, 90, 71, 113, 114, 115,
+    62, 97, 98, 99, 67, 93, 125, 91,
+    126, 72, 116, 94, 63, 95, 100, 107,
+    104, 77, 68, 103, 105, 122, 128, 73,
+    130, 127, 129, 64, 117, 133, 134, 96,
+    108, 78, 135, 101, 109, 110, 69, 131,
+    74, 106, 65, 81, 136, 79, 70, 82,
+    111, 75, 83, 84, 132, 137, 80, 85,
+    112, 86, 138,
 )
 
 
@@ -193,16 +193,23 @@
         device_id_type=MESH,
     )
     swap_copy.start()
+    near = (1, 7, 2, 6, 3, 5, 4)
+    a_z, b_z, c_x, tok_in, ups_in = (links.group() for _ in range(5))
+    own_rows, other_rows = mine_rows, pl.ds(pl.multiple_of((1 - c) * 32, 32), 32)
+
+    def start(group, m, targets, rows):
+        ref = full.at[m, home, z, rows]
+        for target in targets:
+            links.send(group, ref, ref, target)
+
+    along_z, along_x = [to_z(d) for d in near], [to_x(d) for d in (1, 3, 2)]
+    start(a_z, 0, along_z, own_rows)
+    start(c_x, 2, along_x, own_rows)
     swap_copy.wait_recv()
-    near = (1, 7, 2, 6, 3, 5, 4)
-    block0, block1, block2 = (full.at[m, home, z] for m in range(3))
-    a_z, b_z, c_x, tok_in, ups_in = (links.group() for _ in range(5))
-    for d in near:
-        links.send(a_z, block0, block0, to_z(d))
-    for d in (1, 3, 2):
-        links.send(c_x, block2, block2, to_x(d))
-    for d in near:
-        links.send(b_z, block1, block1, to_z(d))
+    start(a_z, 0, along_z, other_rows)
+    start(c_x, 2, along_x, other_rows)
+    start(b_z, 1, along_z, own_rows)
+    start(b_z, 1, along_z, other_rows)
     links.send(tok_in, tokens, tok.at[pl.ds(TOK, TOK)], sibling, 1)
     links.send(ups_in, upstream, ups.at[pl.ds(TOK, TOK)], sibling, 2)
 

time: 83.5 us -> 80.2 us (0.960); the launches traced: 82.5 us -> 80.1 us
  Pallas kernels: 81 us -> 78.5 us
    pallas_call x1, Pallas kernels: 81 us -> 78.5 us  [on_device(): pl.pallas_call(kernel, out_shape=jax.ShapeDtypeStruct((3, 16, COLS), F32)...]
where the time goes in v4:
time: 80.2 us; the launch traced here: 80.1 us
  Pallas kernels  78.5 us (98%)
  local copies, waits for them, and re-layouts  1.54 us (2%)
    pallas_call x1, Pallas kernels, on_device(): pl.pallas_call(kernel, out_shape=jax.ShapeDtypeStruct((3, 16, COLS), F32)...  78.5 us

profile of v4, /device:TPU:32, one launch (start us, length us, event | category | flops | bytes accessed | tf_op | source)
XLA Modules:
  0.0 80.1 jit_solution(641109755404509088)
XLA Ops:
  0.0 78.5 %bucket_grads.1 = f32[3,16,512]{2,1,0:T(8,128)} custom-call(bf16[256,8192]{1,0:T(8,128)(2,1)} %tokens.1, bf16[256,8192]{1,0:T(8,128)(2,1)} %upstream.1, bf16[3,32,256]{2,1,0:T(8,128)(2,1)} %shard_hbm.1), custom_call_target="tpu_custom_call" | custom-call | tf_op jit(solution)/shard_map/bucket_grads/pallas_call | solution.py:556
  78.6 1.5 %copy.5 = f32[3,16,512]{2,1,0:T(8,128)} copy(f32[3,16,512]{2,1,0:T(8,128)} %bucket_grads.1) | data formatting | bytes 196608

commit v5 on v4

--- a/solution.py
+++ b/solution.py
@@ -193,7 +193,7 @@
         device_id_type=MESH,
     )
     swap_copy.start()
-    near = (1, 7, 2, 6, 3, 5, 4)
+    near = (4, 3, 5, 2, 6, 1, 7)
     a_z, b_z, c_x, tok_in, ups_in = (links.group() for _ in range(5))
     own_rows, other_rows = mine_rows, pl.ds(pl.multiple_of((1 - c) * 32, 32), 32)
 
@@ -203,8 +203,8 @@
             links.send(group, ref, ref, target)
 
     along_z, along_x = [to_z(d) for d in near], [to_x(d) for d in (1, 3, 2)]
+    start(c_x, 2, along_x, own_rows)
     start(a_z, 0, along_z, own_rows)
-    start(c_x, 2, along_x, own_rows)
     swap_copy.wait_recv()
     start(a_z, 0, along_z, other_rows)
     start(c_x, 2, along_x, other_rows)

time: 80.2 us -> 80.4 us (level); the launches traced: 80.1 us -> 79.4 us
  no operation moved by 1% of the time
where the time goes in v5:
time: 80.4 us; the launch traced here: 79.4 us
  Pallas kernels  77.9 us (97%)
  local copies, waits for them, and re-layouts  1.54 us (2%)
    pallas_call x1, Pallas kernels, on_device(): pl.pallas_call(kernel, out_shape=jax.ShapeDtypeStruct((3, 16, COLS), F32)...  77.9 us

profile of v5, /device:TPU:32, one launch (start us, length us, event | category | flops | bytes accessed | tf_op | source)
XLA Modules:
  0.0 79.4 jit_solution(1026957094843315860)
XLA Ops:
  0.0 77.9 %bucket_grads.1 = f32[3,16,512]{2,1,0:T(8,128)} custom-call(bf16[256,8192]{1,0:T(8,128)(2,1)} %tokens.1, bf16[256,8192]{1,0:T(8,128)(2,1)} %upstream.1, bf16[3,32,256]{2,1,0:T(8,128)(2,1)} %shard_hbm.1), custom_call_target="tpu_custom_call" | custom-call | tf_op jit(solution)/shard_map/bucket_grads/pallas_call | solution.py:556
  77.9 1.5 %copy.5 = f32[3,16,512]{2,1,0:T(8,128)} copy(f32[3,16,512]{2,1,0:T(8,128)} %bucket_grads.1) | data formatting | bytes 196608
